TPU v7x, 512 devices: a whole 4x4x16 slice. The times are simulated.
512 devices in a mesh: head: 8 (over y, x_hi), seq: 64 (over z, x_lo, core).
Axes of the slice: x: 4 (x_hi: 2, x_lo: 2; x = x_hi * 2 + x_lo), y: 4, z: 16, core: 2. Of those that a mesh axis runs over, the one named last changes fastest.
Arguments:
- tokens: bfloat16 [49152, 2048], P('seq', 'head'), may hold values from -6 to 6
- weights: bfloat16 [3, 2048, 2048], P(None, 'seq', 'head'), may hold values from -0.06591797 to 0.06591797
- landmark_pos: int32 [16, 256], P('head'), may hold values from 0 to 49151, as said below
Outputs:
- attended: bfloat16 [49152, 2048], P('seq', 'head')
Inputs may be any that keep to these rules, and one draw needn't show every extreme that they name: `landmark_pos`: landmark number j of every head lies in tokens j * 192 to (j + 1) * 192 - 1.
All inputs are finite; a program needn't handle non-finite values. Where the computation divides by a largest or mean magnitude, that divisor is 1e-20 or more.
Results may differ from a plain program's by a relative error of at most 0.0041.
Values may be sent and summed in bfloat16 or wider, within the bound.
No kernel may reach another device: no remote copies, remote signals or barrier semaphores. Data moves between devices by JAX's collectives and lax.ppermute only.
A program may use at most 64 MiB of HBM per device.

v0:
```python
import math
import jax
import jax.numpy as jnp
from jax import lax
from jax.sharding import PartitionSpec as P

NSTEPS = 6


def gauss(left, right):
    inner = jnp.einsum("hie,hje->hij", left, right, preferred_element_type=jnp.float32)
    left32 = left.astype(jnp.float32)
    right32 = right.astype(jnp.float32)
    dist = (
        jnp.sum(left32 * left32, -1)[:, :, None]
        + jnp.sum(right32 * right32, -1)[:, None, :]
        - 2.0 * inner
    )
    return jnp.exp(-dist / (2.0 * math.sqrt(left.shape[-1])))


def batched(left, right):
    return jnp.einsum("hij,hjk->hik", left, right, precision=lax.Precision.HIGHEST)


def gather_landmarks(query, keys, landmark_pos):
    per_group = landmark_pos.shape[1] // lax.axis_size("seq")
    tok_rows = query.shape[1]
    group = lax.axis_index("seq")
    local_pos = lax.dynamic_slice_in_dim(landmark_pos, group * per_group, per_group, 1)
    offsets = local_pos - group * tok_rows
    picker = (offsets[:, :, None] == jnp.arange(tok_rows, dtype=jnp.int32)[None, None, :]).astype(
        jnp.bfloat16
    )
    picked_q = jnp.einsum("hjt,hte->hje", picker, query, preferred_element_type=jnp.float32)
    picked_k = jnp.einsum("hjt,hte->hje", picker, keys, preferred_element_type=jnp.float32)
    number = group * per_group + jnp.arange(per_group, dtype=jnp.int32)
    even = (number % 2 == 0)[None, :, None]
    local_marks = jnp.where(even, picked_q, picked_k).astype(jnp.bfloat16)
    return lax.all_gather(local_marks, "seq", axis=1, tiled=True)


def shards(tokens, weights, landmark_pos):
    tok_rows = tokens.shape[0]
    heads_dev = landmark_pos.shape[0]
    head_cols = weights.shape[2]
    head_size = head_cols // heads_dev
    whole = lax.all_gather(tokens, "head", axis=1, tiled=True)

    def heads_of(flat):
        return jnp.transpose(
            flat.astype(jnp.bfloat16).reshape(tok_rows, heads_dev, head_size), (1, 0, 2)
        )

    projected = jnp.einsum(
        "td,kdc->ktc",
        whole,
        lax.all_gather(weights, "seq", axis=1, tiled=True),
        preferred_element_type=jnp.float32,
    )
    query = heads_of(projected[0])
    keys = heads_of(projected[1])
    values = heads_of(projected[2])
    landmarks = gather_landmarks(query, keys, landmark_pos)
    key_weights = gauss(landmarks, keys).astype(jnp.bfloat16)
    partial_sum = jnp.einsum(
        "hjt,hte->hje", key_weights, values, preferred_element_type=jnp.float32
    )
    summary = lax.psum(partial_sum, "seq")
    inner = gauss(landmarks, landmarks)
    scale_cols = jnp.max(jnp.sum(jnp.abs(inner), 1), axis=-1)
    scale_rows = jnp.max(jnp.sum(jnp.abs(inner), 2), axis=-1)
    iterate = inner / (scale_cols * scale_rows)[:, None, None]
    for step in range(NSTEPS):
        iterate = 2.0 * iterate - batched(batched(iterate, inner), iterate)
    mixed = batched(iterate, summary).astype(jnp.bfloat16)
    query_weights = gauss(query, landmarks).astype(jnp.bfloat16)
    result = jnp.einsum("htm,hme->the", query_weights, mixed, preferred_element_type=jnp.float32)
    return result.reshape(tok_rows, head_cols).astype(jnp.bfloat16)


def solution(mesh):
    return jax.shard_map(
        shards,
        mesh=mesh,
        in_specs=(P("seq", "head"), P(None, "seq", "head"), P("head", None)),
        out_specs=P("seq", "head"),
        check_vma=False,
    )
```

profile of v0, /device:TPU:1, one launch (start us, length us, event | category | flops | bytes accessed | tf_op | source)
XLA Modules:
  0.0 707.9 jit_solution(10493289057307640920)
XLA Ops:
  6.5 0.0 all-gather.5.cloned.1.call-start
  6.5 0.7 all-gather.5.cloned.1.call-update
  7.3 0.0 all-gather.3.cloned.1.call-start
  7.3 0.7 all-gather.3.cloned.1.call-update
  8.0 0.0 all-reduce.2.cloned.1.call-start
  8.1 0.8 dynamic-slice_subtract_fusion
  8.8 85.7 %all-gather.5.cloned.1.call-done = bf16[768,2048]{1,0:T(8,128)(2,1)} async-done(((bf16[768,256]{1,0:T(8,128)(2,1)}), bf16[768,2048]{1,0:T(8,128)(2,1)}) %all-gather.5.cloned.1.call-update) | async-done | bytes 3145744 | tf_op jit(solution)/shard_map/all_gather | solution.py:48
  94.6 124.4 %all-gather.3.cloned.1.call-done = bf16[3,2048,256]{2,1,0:T(8,128)(2,1)} async-done(((bf16[3,32,256]{2,1,0:T(8,128)(2,1)}), bf16[3,2048,256]{2,1,0:T(8,128)(2,1)}) %all-gather.3.cloned.1.call-update) | async-done | bytes 3145744 | tf_op jit(solution)/shard_map/all_gather | solution.py:58
  219.0 5.5 fusion.5
  224.5 0.1 fusion.51
  224.6 0.2 copy.27
  224.8 0.3 multiply_reduce_fusion
  225.1 0.2 fusion.33
  225.3 0.2 copy.28
  225.6 0.3 multiply_reduce_fusion.1
  225.9 0.2 fusion.15
  226.1 62.3 %all_gather.11 = bf16[2,256,128]{2,0,1:T(2,128)(2,1)S(1)} all-gather(bf16[2,4,128]{2,0,1:T(2,128)(2,1)S(1)} %copy.29), channel_id=1, replica_groups=mesh['head'=8,'seq'=64] {'seq'}, dimensions={1}, use_global_device_ids=true | all-gather | bytes 133120 | tf_op jit(solution)/shard_map/all_gather | solution.py:40
  288.4 0.3 multiply_reduce_fusion.2
  288.7 0.1 copy.30
  288.8 0.4 fusion.50
  289.2 0.1 reduce_max.18
  289.4 0.1 reduce_max.19
  289.5 0.7 fusion.24
  290.2 0.8 convolution_subtract_fusion.5
  291.0 0.7 fusion.52
  291.6 0.7 convolution_subtract_fusion.4
  292.3 0.7 fusion.53
  293.0 0.7 convolution_subtract_fusion.3
  293.6 0.7 fusion.54
  294.3 0.7 convolution_subtract_fusion.2
  295.0 0.7 fusion.55
  295.6 0.7 convolution_subtract_fusion.1
  296.3 0.7 fusion.56
  297.0 0.2 copy.36
  297.2 1.5 fusion.8
  298.7 0.0 all-reduce.2.cloned.1.call-update
  298.7 0.7 convolution_subtract_fusion
  299.4 398.6 %all-reduce.2.cloned.1.call-done = f32[2,256,128]{2,1,0:T(8,128)} async-done(((f32[2,256,128]{2,1,0:T(8,128)}), f32[2,256,128]{2,1,0:T(8,128)}) %all-reduce.2.cloned.1.call-update) | async-done | bytes 262160 | tf_op jit(solution)/shard_map/psum | solution.py:69
  698.0 1.6 convolution_convert_fusion
  699.6 0.8 fusion.10
  700.4 0.9 copy.40
  (3 shorter events, 0.0 us)
Async XLA Ops:
  6.5 88.0 %all-gather.5.cloned.1.call-start = ((), (), s32[]{:S(2)}) async-start(), calls=%async_computation.1 | async-start | bytes 3538944 | tf_op jit(solution)/shard_map/all_gather | solution.py:48
  7.3 211.7 %all-gather.3.cloned.1.call-start = ((), (), s32[]{:S(2)}) async-start(), calls=%async_computation | async-start | bytes 3194880 | tf_op jit(solution)/shard_map/all_gather | solution.py:58
  8.0 690.0 %all-reduce.2.cloned.1.call-start = ((), (), s32[]{:S(2)}) async-start(), calls=%async_computation.2 | async-start | bytes 524288 | tf_op jit(solution)/shard_map/psum | solution.py:69
Sparse Core Ops, SparseCore 0:
  10.4 84.1 all-gather.4
  96.7 122.2 all-gather.2
  298.9 399.1 all-reduce.1
where the time goes:
time: 708 us
  waiting for transfers between devices  610 us (86%)
  blocking collectives  62.3 us (9%)
  matrix products  18.2 us (3%)
  between operations  13.3 us (2%)
    psum x1, waiting for transfers between devices, shards(): summary = lax.psum(partial_sum, 'seq')  399 us
    all_gather x1, waiting for transfers between devices, shards(): lax.all_gather(weights, 'seq', axis=1, tiled=True)  124 us
    all_gather x1, waiting for transfers between devices, shards(): whole = lax.all_gather(tokens, 'head', axis=1, tiled=True)  85.7 us
    all_gather x1, blocking collectives, gather_landmarks(): return lax.all_gather(local_marks, 'seq', axis=1, tiled=True)  62.3 us
  transfers between devices with their start and end apart: 3, of which 3 were waited for; matrix products, arithmetic and copies ran while one was open for 0% of the time, Pallas kernels for 0%

commit v1 on v0

--- a/solution.py
+++ b/solution.py
@@ -66,7 +66,7 @@
     partial_sum = jnp.einsum(
         "hjt,hte->hje", key_weights, values, preferred_element_type=jnp.float32
     )
-    summary = lax.psum(partial_sum, "seq")
+    summary = jnp.sum(lax.all_gather(partial_sum, "seq"), axis=0)
     inner = gauss(landmarks, landmarks)
     scale_cols = jnp.max(jnp.sum(jnp.abs(inner), 1), axis=-1)
     scale_rows = jnp.max(jnp.sum(jnp.abs(inner), 2), axis=-1)

time: 708 us -> 442 us (0.62)
  waiting for transfers between devices: 610 us -> 339 us
    psum x1 -> x0, waiting for transfers between devices: 399 us -> none  [shards(): summary = lax.psum(partial_sum, 'seq')]
    all_gather x0 -> x1, waiting for transfers between devices: none -> 127 us  [shards(): summary = jnp.sum(lax.all_gather(partial_sum, 'seq'), axis=0)]
  transfers between devices with their start and end apart: 3 -> 3, of which waited for: 3 -> 3; matrix products, arithmetic and copies ran while one was open for 0% -> 2% of each run, Pallas kernels for 0% -> 0%
where the time goes in v1:
time: 442 us
  waiting for transfers between devices  339 us (77%)
  blocking collectives  62.3 us (14%)
  matrix products  17.3 us (4%)
  between operations  13.3 us (3%)
  other arithmetic  8.5 us (2%)
    all_gather x1, waiting for transfers between devices, shards(): summary = jnp.sum(lax.all_gather(partial_sum, 'seq'), axis=0)  127 us
    all_gather x1, waiting for transfers between devices, shards(): lax.all_gather(weights, 'seq', axis=1, tiled=True)  124 us
    all_gather x1, waiting for transfers between devices, shards(): whole = lax.all_gather(tokens, 'head', axis=1, tiled=True)  85.7 us
    all_gather x1, blocking collectives, gather_landmarks(): return lax.all_gather(local_marks, 'seq', axis=1, tiled=True)  62.3 us
  transfers between devices with their start and end apart: 3, of which 3 were waited for; matrix products, arithmetic and copies ran while one was open for 2% of the time, Pallas kernels for 0%

profile of v1, /device:TPU:1, one launch (start us, length us, event | category | flops | bytes accessed | tf_op | source)
XLA Modules:
  0.0 442.0 jit_solution(5104217001340310524)
XLA Ops:
  6.5 0.0 all-gather.7.cloned.1.call-start
  6.5 0.7 all-gather.7.cloned.1.call-update
  7.3 0.0 all-gather.5.cloned.1.call-start
  7.3 0.7 all-gather.5.cloned.1.call-update
  8.0 0.0 all-gather.9.cloned.1.call-start
  8.1 0.8 dynamic-slice_subtract_fusion
  8.8 85.7 %all-gather.7.cloned.1.call-done = bf16[768,2048]{1,0:T(8,128)(2,1)} async-done(((bf16[768,256]{1,0:T(8,128)(2,1)}), bf16[768,2048]{1,0:T(8,128)(2,1)}) %all-gather.7.cloned.1.call-update) | async-done | bytes 3145744 | tf_op jit(solution)/shard_map/all_gather | solution.py:48
  94.6 124.4 %all-gather.5.cloned.1.call-done = bf16[3,2048,256]{2,1,0:T(8,128)(2,1)} async-done(((bf16[3,32,256]{2,1,0:T(8,128)(2,1)}), bf16[3,2048,256]{2,1,0:T(8,128)(2,1)}) %all-gather.5.cloned.1.call-update) | async-done | bytes 3145744 | tf_op jit(solution)/shard_map/all_gather | solution.py:58
  219.0 5.5 %fusion.5 = bf16[3,768,256]{1,2,0:T(8,128)(2,1)S(1)} fusion(bf16[3,2048,256]{2,1,0:T(8,128)(2,1)} %all-gather.5.cloned.1.call-done, bf16[768,2048]{1,0:T(8,128)(2,1)} %all-gather.7.cloned.1.call-done), kind=kOutput, calls=%fused_computation.5 | convolution fusion | flops 2416508928 | bytes 7471104 | tf_op jit(solution)/shard_map/td,kdc->ktc/dot_general | solution.py:55
  224.5 0.1 fusion.51
  224.6 0.2 copy.29
  224.8 0.2 copy.30
  225.1 0.3 multiply_reduce_fusion.1
  225.4 0.2 fusion.33
  225.6 0.2 fusion.15
  225.8 62.3 %all_gather.17 = bf16[2,256,128]{2,0,1:T(2,128)(2,1)S(1)} all-gather(bf16[2,4,128]{2,0,1:T(2,128)(2,1)S(1)} %copy.31), channel_id=1, replica_groups=mesh['head'=8,'seq'=64] {'seq'}, dimensions={1}, use_global_device_ids=true | all-gather | bytes 133120 | tf_op jit(solution)/shard_map/all_gather | solution.py:40
  288.1 0.3 multiply_reduce_fusion.2
  288.5 0.1 copy.32
  288.5 0.2 copy.38
  288.8 1.5 fusion.8
  290.2 0.0 all-gather.9.cloned.1.call-update
  290.3 0.4 fusion.50
  290.7 0.1 reduce_max.18
  290.8 0.1 reduce_max.19
  290.9 0.3 multiply_reduce_fusion
  291.2 0.7 fusion.24
  291.9 0.8 convolution_subtract_fusion.5
  292.7 0.7 fusion.52
  293.3 0.7 convolution_subtract_fusion.4
  294.0 0.7 fusion.53
  294.7 0.7 convolution_subtract_fusion.3
  295.4 0.7 fusion.54
  296.0 0.7 convolution_subtract_fusion.2
  296.7 0.7 fusion.55
  297.4 0.7 convolution_subtract_fusion.1
  298.0 0.7 fusion.56
  298.7 0.7 convolution_subtract_fusion
  299.4 127.2 %all-gather.9.cloned.1.call-done = f32[128,256,128]{2,1,0:T(8,128)} async-done(((f32[2,256,128]{2,1,0:T(8,128)}), f32[128,256,128]{2,1,0:T(8,128)}) %all-gather.9.cloned.1.call-update) | async-done | bytes 16777232 | tf_op jit(solution)/shard_map/all_gather | solution.py:69
  426.6 6.6 %reduce_sum.58 = f32[2,256,128]{2,1,0:T(8,128)S(1)} reduce(f32[64,2,256,128]{3,2,1,0:T(8,128)} %bitcast.59, f32[]{:T(128)} %constant.38.clone.1), dimensions={0}, to_apply=%region_6.7 | reduce | flops 4128768 | bytes 17039364 | tf_op jit(solution)/shard_map/reduce_sum | solution.py:69
  433.1 0.6 convolution_convert_fusion
  433.7 0.8 fusion.10
  434.5 0.9 copy.42
  (3 shorter events, 0.0 us)
Async XLA Ops:
  6.5 88.0 %all-gather.7.cloned.1.call-start = ((), (), s32[]{:S(2)}) async-start(), calls=%async_computation.1 | async-start | bytes 3538944 | tf_op jit(solution)/shard_map/all_gather | solution.py:48
  7.3 211.7 %all-gather.5.cloned.1.call-start = ((), (), s32[]{:S(2)}) async-start(), calls=%async_computation | async-start | bytes 3194880 | tf_op jit(solution)/shard_map/all_gather | solution.py:58
  8.0 418.6 %all-gather.9.cloned.1.call-start = ((), (), s32[]{:S(2)}) async-start(), calls=%async_computation.2 | async-start | bytes 17039360 | tf_op jit(solution)/shard_map/all_gather | solution.py:69
Sparse Core Ops, SparseCore 0:
  10.4 84.1 all-gather.6
  96.7 122.2 all-gather.4
  290.4 136.1 all-gather.8

commit v2 on v0

--- a/solution.py
+++ b/solution.py
@@ -45,7 +45,9 @@
     heads_dev = landmark_pos.shape[0]
     head_cols = weights.shape[2]
     head_size = head_cols // heads_dev
-    whole = lax.all_gather(tokens, "head", axis=1, tiled=True)
+    whole = jnp.concatenate(
+        lax.all_to_all(jnp.stack([tokens] * lax.axis_size("head")), "head", 0, 0), axis=1
+    )
 
     def heads_of(flat):
         return jnp.transpose(

time: 708 us -> 619 us (0.87)
  waiting for transfers between devices: 610 us -> 504 us
  local copies, waits for them, and re-layouts: 1.78 us -> 12.4 us
  starting transfers between devices: 0.08 us -> 7.65 us
    all_gather x1 -> x0, waiting for transfers between devices: 85.7 us -> none  [shards(): whole = lax.all_gather(tokens, 'head', axis=1, tiled=True)]
    all_gather x1, waiting for transfers between devices: 124 us -> 73.1 us  [shards(): lax.all_gather(weights, 'seq', axis=1, tiled=True)]
    all_to_all x0 -> x1, waiting for transfers between devices: none -> 40 us  [shards(): lax.all_to_all(jnp.stack([tokens] * lax.axis_size('head')), 'head', 0, 0)]
    psum x1, waiting for transfers between devices: 399 us -> 391 us  [shards(): summary = lax.psum(partial_sum, 'seq')]
    reshape x0 -> x2, local copies, waits for them, and re-layouts: none -> 7.72 us  [shards(): jnp.concatenate(lax.all_to_all(jnp.stack([tokens] * lax.axis_size('head')...]
    all_to_all x0 -> x1, starting transfers between devices: none -> 7.61 us  [shards(): lax.all_to_all(jnp.stack([tokens] * lax.axis_size('head')), 'head', 0, 0)]
  transfers between devices with their start and end apart: 3 -> 3, of which waited for: 3 -> 3; matrix products, arithmetic and copies ran while one was open for 0% -> 3% of each run, Pallas kernels for 0% -> 0%
where the time goes in v2:
time: 619 us
  waiting for transfers between devices  504 us (81%)
  blocking collectives  62.3 us (10%)
  matrix products  17.3 us (3%)
  between operations  13.6 us (2%)
  local copies, waits for them, and re-layouts  12.4 us (2%)
  starting transfers between devices  7.65 us (1%)
    psum x1, waiting for transfers between devices, shards(): summary = lax.psum(partial_sum, 'seq')  391 us
    all_gather x1, waiting for transfers between devices, shards(): lax.all_gather(weights, 'seq', axis=1, tiled=True)  73.1 us
    all_gather x1, blocking collectives, gather_landmarks(): return lax.all_gather(local_marks, 'seq', axis=1, tiled=True)  62.3 us
    all_to_all x1, waiting for transfers between devices, shards(): lax.all_to_all(jnp.stack([tokens] * lax.axis_size('head')), 'head', 0, 0)  40 us
  transfers between devices with their start and end apart: 3, of which 3 were waited for; matrix products, arithmetic and copies ran while one was open for 3% of the time, Pallas kernels for 0%

profile of v2, /device:TPU:1, one launch (start us, length us, event | category | flops | bytes accessed | tf_op | source)
XLA Modules:
  0.0 618.9 jit_solution(4790970774319797903)
XLA Ops:
  6.5 0.0 all-gather.2.cloned.1.call-start
  6.5 0.7 all-gather.2.cloned.1.call-update
  7.3 2.9 stack.2
  10.2 0.0 copy-start
  10.2 7.6 %all-to-all-start = ((bf16[8,768,256]{2,1,0:T(8,128)(2,1)}), bf16[8,768,256]{2,1,0:T(8,128)(2,1)S(1)}, u32[]{:S(2)}, u32[]{:S(2)}) async-start(bf16[8,768,256]{2,1,0:T(8,128)(2,1)} %stack.2), calls=%async_computation | async-start | bytes 6291456 | tf_op jit(solution)/shard_map/all_to_all | solution.py:49
  17.8 0.0 all-reduce.2.cloned.1.call-start
  17.8 0.0 copy-done
  17.8 0.1 dynamic-slice_subtract_fusion
  17.9 40.0 %all-to-all-done = bf16[8,768,256]{2,1,0:T(8,128)(2,1)S(1)} async-done(((bf16[8,768,256]{2,1,0:T(8,128)(2,1)}), bf16[8,768,256]{2,1,0:T(8,128)(2,1)S(1)}, u32[]{:S(2)}, u32[]{:S(2)}) %all-to-all-start) | async-done | bytes 3145760 | tf_op jit(solution)/shard_map/all_to_all | solution.py:49
  57.9 3.5 copy.29
  61.4 4.2 reshape.47
  65.6 73.1 %all-gather.2.cloned.1.call-done = bf16[3,2048,256]{2,1,0:T(8,128)(2,1)} async-done(((bf16[3,32,256]{2,1,0:T(8,128)(2,1)}), bf16[3,2048,256]{2,1,0:T(8,128)(2,1)}) %all-gather.2.cloned.1.call-update) | async-done | bytes 3145744 | tf_op jit(solution)/shard_map/all_gather | solution.py:60
  138.8 4.6 fusion
  143.3 0.1 fusion.44
  143.4 0.2 copy.30
  143.7 0.3 multiply_reduce_fusion
  143.9 0.2 fusion.26
  144.2 0.3 copy.31
  144.4 0.3 multiply_reduce_fusion.1
  144.7 0.2 fusion.8
  144.9 62.3 %all_gather.7 = bf16[2,256,128]{2,0,1:T(2,128)(2,1)S(1)} all-gather(bf16[2,4,128]{2,0,1:T(2,128)(2,1)S(1)} %copy.32), channel_id=1, replica_groups=mesh['head'=8,'seq'=64] {'seq'}, dimensions={1}, use_global_device_ids=true | all-gather | bytes 133120 | tf_op jit(solution)/shard_map/all_gather | solution.py:40
  207.3 0.3 multiply_reduce_fusion.2
  207.6 0.1 copy.33
  207.7 0.2 copy.39
  207.9 0.4 fusion.43
  208.4 1.5 fusion.1
  209.8 0.0 all-reduce.2.cloned.1.call-update
  209.8 0.1 reduce_max.18
  210.0 0.1 reduce_max.19
  210.1 0.7 fusion.17
  210.8 0.8 convolution_subtract_fusion.5
  211.6 0.7 fusion.45
  212.2 0.7 convolution_subtract_fusion.4
  212.9 0.7 fusion.46
  213.6 0.7 convolution_subtract_fusion.3
  214.2 0.7 fusion.47
  214.9 0.7 convolution_subtract_fusion.2
  215.6 0.7 fusion.48
  216.2 0.7 convolution_subtract_fusion.1
  216.9 0.7 fusion.49
  217.6 0.7 convolution_subtract_fusion
  218.3 390.5 %all-reduce.2.cloned.1.call-done = f32[2,256,128]{2,1,0:T(8,128)} async-done(((f32[2,256,128]{2,1,0:T(8,128)}), f32[2,256,128]{2,1,0:T(8,128)}) %all-reduce.2.cloned.1.call-update) | async-done | bytes 262160 | tf_op jit(solution)/shard_map/psum | solution.py:71
  608.8 1.6 convolution_convert_fusion.1
  610.4 0.8 fusion.3
  611.2 0.9 copy.43
  (3 shorter events, 0.0 us)
Async XLA Ops:
  6.5 132.2 %all-gather.2.cloned.1.call-start = ((), (), s32[]{:S(2)}) async-start(), calls=%async_computation.1 | async-start | bytes 3194880 | tf_op jit(solution)/shard_map/all_gather | solution.py:60
  10.2 7.7 %copy-start = (s32[2,256]{1,0:T(2,128)S(1)}, s32[2,256]{1,0:T(2,128)}, u32[]{:S(2)}) copy-start(s32[2,256]{1,0:T(2,128)} %param.5) | copy-start | bytes 6148
  10.2 47.7 %all-to-all-start = ((bf16[8,768,256]{2,1,0:T(8,128)(2,1)}), bf16[8,768,256]{2,1,0:T(8,128)(2,1)S(1)}, u32[]{:S(2)}, u32[]{:S(2)}) async-start(bf16[8,768,256]{2,1,0:T(8,128)(2,1)} %stack.2), calls=%async_computation | async-start | bytes 6291456 | tf_op jit(solution)/shard_map/all_to_all | solution.py:49
  17.8 591.0 %all-reduce.2.cloned.1.call-start = ((), (), s32[]{:S(2)}) async-start(), calls=%async_computation.2 | async-start | bytes 524288 | tf_op jit(solution)/shard_map/psum | solution.py:71
Sparse Core Ops, SparseCore 0:
  9.5 129.1 all-gather.1
  210.0 398.8 all-reduce.1
